TPU v7x, 256 devices: a whole 4x4x8 slice. The times are simulated.
256 devices in a mesh: blk: 64 (over y, x, z_hi, core), grp: 4 (over z_lo).
Axes of the slice: x: 4, y: 4, z: 8 (z_hi: 2, z_lo: 4; z = z_hi * 4 + z_lo), core: 2. Of those that a mesh axis runs over, the one named last changes fastest.
Arguments:
- amplitudes: float32 [2048, 4, 65536], P('grp', None, 'blk'), may hold values from -6 to 6
- integrals: float32 [4, 65536, 256], P('grp', 'blk'), may hold values from -0.0234375 to 0.0234375
- irrep_sizes: int32 [4], replicated, may hold values from 86 to 256, as said below
- owner_map: int32 [4], replicated, may hold values from 0 to 3, each once
Outputs:
- ladder: float32 [2048, 4, 256], P('grp', None, 'blk')
Inputs may be any that keep to these rules, and one draw needn't show every extreme that they name: `irrep_sizes`: one irrep fills its block and one has the smallest size.
All inputs are finite; a program needn't handle non-finite values.
Results may differ from a plain program's by a relative error of at most 0.0001.
Values sent between devices are 32-bit elements; how exact they have to be, the bound alone decides.
No kernel may reach another device: no remote copies, remote signals or barrier semaphores. Data moves between devices by JAX's collectives and lax.ppermute only.
A program may use at most 128 MiB of HBM per device.

v0:
```python
import jax
import jax.numpy as jnp
from jax import lax
from jax.sharding import PartitionSpec as P

BLOCK = 256
IRREPS = 4


def from_root(shard, axis, root):
    mine = lax.axis_index(axis) == root
    return lax.psum(jnp.where(mine, shard, jnp.zeros_like(shard)), axis)


def slot_valid(irrep_sizes, offset, width):
    slot = offset + jnp.arange(width, dtype=jnp.int32)
    sizes = irrep_sizes[:, None]
    return ((slot[None, :] // BLOCK < sizes) & (slot[None, :] % BLOCK < sizes)).astype(jnp.float32)


def local(amplitudes, integrals, irrep_sizes, owner_map):
    slot_width = amplitudes.shape[2]
    column_width = integrals.shape[2] // lax.axis_size("blk")
    position = lax.axis_index("blk")
    row_valid = slot_valid(irrep_sizes, position * slot_width, slot_width)
    column_valid = slot_valid(irrep_sizes, position * column_width, column_width)
    masked = amplitudes * row_valid[None, :, :]
    blocks = []
    for irrep in range(IRREPS):
        slab_rows = from_root(integrals, "grp", owner_map[irrep])[0]
        blocks.append(
            jnp.dot(
                masked[:, irrep, :],
                slab_rows,
                precision=lax.Precision.HIGHEST,
                preferred_element_type=jnp.float32,
            )
        )
    partial_value = jnp.stack(blocks, axis=1)
    result = lax.psum_scatter(partial_value, "blk", scatter_dimension=2, tiled=True)
    return result * column_valid[None, :, :]


def solution(mesh):
    in_specs = (P("grp", None, "blk"), P("grp", "blk", None), P(), P())
    out_specs = P("grp", None, "blk")
    return jax.shard_map(local, mesh=mesh, in_specs=in_specs, out_specs=out_specs, check_vma=False)
```

profile of v0, /device:TPU:1, one launch (start us, length us, event | category | flops | bytes accessed | tf_op | source)
XLA Modules:
  0.0 1000.0 jit_solution(15541328283892642709)
XLA Ops:
  6.5 0.0 all-reduce.7.cloned.1.call-start
  6.5 1.4 fusion.13
  10.5 3.3 select_bitcast_fusion.3
  13.7 0.0 copy-start.3
  13.7 0.0 all-reduce.7.cloned.1.call-update
  13.7 0.0 all-reduce.5.cloned.1.call-start
  13.8 0.6 copy-done.3
  14.4 0.1 and_convert_fusion
  14.4 11.5 %copy_multiply_fusion = f32[512,4,1024]{2,0,1:T(8,128)} fusion(f32[512,4,1024]{2,1,0:T(4,128)} %param.4, f32[4,1024]{1,0:T(4,128)S(1)} %and_convert_fusion), kind=kLoop, calls=%fused_computation | loop fusion | flops 2097152 | bytes 16793600 | tf_op jit(solution)/shard_map/mul | solution.py:27
  25.9 156.1 %all-reduce.7.cloned.1.call-done = (f32[1024,256]{1,0:T(8,128)}, f32[1024,256]{1,0:T(8,128)}, f32[1024,256]{1,0:T(8,128)}, f32[1024,256]{1,0:T(8,128)}) async-done(((f32[1024,256]{1,0:T(8,128)}, f32[1024,256]{1,0:T(8,128)}, f32[1024,256]{1,0:T(8,128)}, f32[1024,256]{1,0:T(8,128)}), (f32[1024,256]{1,0:T(8,128)}, f32[1024,256]{1,0:T(8,128)}, f32[1024,256]{1,0:T(8,128)}, ...) | async-done | bytes 4194320 | tf_op jit(solution)/shard_map/psum | solution.py:12
  182.0 0.0 copy-start.2
  182.0 3.7 fusion.4
  185.7 0.0 copy-start.1
  185.7 0.0 copy-done.2
  185.8 3.5 fusion.5
  189.2 0.0 copy-start
  189.3 0.0 copy-done.1
  189.3 3.5 fusion.6
  192.8 0.0 copy-done
  192.8 3.4 fusion.7
  196.2 0.1 pad_maximum_fusion
  196.3 2.0 copy.9
  198.3 0.0 copy-start.4
  198.3 0.0 all-reduce.5.cloned.1.call-update
  198.4 0.6 copy-done.4
  199.0 0.6 dynamic-slice
  200.3 0.1 and_convert_fusion.1
  200.3 791.4 %all-reduce.5.cloned.1.call-done = f32[512,4,256]{0,1,2:T(4,128)} async-done(((f32[512,4,256]{0,1,2:T(4,128)}), f32[512,4,256]{0,1,2:T(4,128)}) %all-reduce.5.cloned.1.call-update) | async-done | bytes 2097168
  991.7 0.8 dynamic-slice_multiply_fusion
  992.6 0.6 copy.10
  (2 shorter events, 0.0 us)
Async XLA Ops:
  6.5 175.5 %all-reduce.7.cloned.1.call-start = ((), (), s32[]{:S(2)}) async-start(), calls=%async_computation.1 | async-start | bytes 8388608 | tf_op jit(solution)/shard_map/psum | solution.py:12
  13.7 0.7 copy-start.3
  13.7 978.0 %all-reduce.5.cloned.1.call-start = ((), (), s32[]{:S(2)}) async-start(), calls=%async_computation | async-start | bytes 4194304
  182.0 3.8 copy-start.2
  185.7 3.5 copy-start.1
  189.2 3.5 copy-start
  198.3 0.7 copy-start.4
Sparse Core Ops, SparseCore 0:
  13.9 168.0 all-reduce.6
  198.5 793.2 all-reduce.4
where the time goes:
time: 1000 us
  waiting for transfers between devices  948 us (95%)
  between operations  16.6 us (2%)
  other arithmetic  15.9 us (2%)
  matrix products  14.1 us (1%)
    unnamed x3, waiting for transfers between devices  791 us
    psum x1, waiting for transfers between devices, from_root(): return lax.psum(jnp.where(mine, shard, jnp.zeros_like(shard)), axis)  156 us
  transfers between devices with their start and end apart: 2, of which 2 were waited for; matrix products, arithmetic and copies ran while one was open for 1% of the time, Pallas kernels for 0%

commit v1 on v0

--- a/solution.py
+++ b/solution.py
@@ -7,9 +7,15 @@
 IRREPS = 4
 
 
+def add_all(x, axis):
+    parts = lax.all_gather(x, axis, axis=0, tiled=False)
+    result = parts.sum(axis=0)
+    return result
+
+
 def from_root(shard, axis, root):
     mine = lax.axis_index(axis) == root
-    return lax.psum(jnp.where(mine, shard, jnp.zeros_like(shard)), axis)
+    return add_all(jnp.where(mine, shard, jnp.zeros_like(shard)), axis)
 
 
 def slot_valid(irrep_sizes, offset, width):

time: 1000 us -> 1170 us (1.17)
  waiting for transfers between devices: 948 us -> 1110 us
    all_gather x0 -> x4, waiting for transfers between devices: none -> 312 us  [add_all(): parts = lax.all_gather(x, axis, axis=0, tiled=False)]
    psum x1 -> x0, waiting for transfers between devices: 156 us -> none  [from_root(): return lax.psum(jnp.where(mine, shard, jnp.zeros_like(shard)), axis)]
    unnamed x3 -> x6, waiting for transfers between devices: 791 us -> 793 us
  transfers between devices with their start and end apart: 2 -> 5, of which waited for: 2 -> 5; matrix products, arithmetic and copies ran while one was open for 1% -> 3% of each run, Pallas kernels for 0% -> 0%
where the time goes in v1:
time: 1170 us
  waiting for transfers between devices  1110 us (95%)
  other arithmetic  26.3 us (2%)
  between operations  16.5 us (1%)
  matrix products  15.5 us (1%)
    unnamed x6, waiting for transfers between devices  793 us
    all_gather x4, waiting for transfers between devices, add_all(): parts = lax.all_gather(x, axis, axis=0, tiled=False)  312 us
  transfers between devices with their start and end apart: 5, of which 5 were waited for; matrix products, arithmetic and copies ran while one was open for 3% of the time, Pallas kernels for 0%

profile of v1, /device:TPU:1, one launch (start us, length us, event | category | flops | bytes accessed | tf_op | source)
XLA Modules:
  0.0 1169.0 jit_solution(7144266580854369798)
XLA Ops:
  6.5 0.0 all-gather.11.cloned.1.call-start
  6.5 1.5 fusion.13
  10.6 3.3 broadcast_select_fusion.3
  13.9 0.0 copy-start.2
  13.9 0.0 all-gather.11.cloned.1.call-update
  14.0 0.0 all-gather.15.cloned.1.call-start
  14.0 0.7 all-gather.15.cloned.1.call-update
  14.7 0.0 all-gather.13.cloned.1.call-start
  14.8 0.7 all-gather.13.cloned.1.call-update
  15.4 0.0 all-gather.9.cloned.1.call-start
  15.5 0.5 all-gather.9.cloned.1.call-update
  16.0 0.0 all-reduce.3.cloned.1.call-start
  16.1 0.0 copy-done.2
  16.1 0.1 and_convert_fusion
  16.2 11.5 copy_multiply_fusion
  27.6 74.0 %all-gather.11.cloned.1.call-done = f32[4,1024,256]{2,1,0:T(8,128)} async-done(((f32[1,1024,256]{2,1,0:T(8,128)}), f32[4,1024,256]{2,1,0:T(8,128)}) %all-gather.11.cloned.1.call-update) | async-done | bytes 4194320 | tf_op jit(solution)/shard_map/all_gather | solution.py:11
  101.6 2.6 reduce.5
  104.2 83.3 %all-gather.15.cloned.1.call-done = f32[4,1024,256]{2,1,0:T(8,128)} async-done(((f32[1,1024,256]{2,1,0:T(8,128)}), f32[4,1024,256]{2,1,0:T(8,128)}) %all-gather.15.cloned.1.call-update) | async-done | bytes 4194320 | tf_op jit(solution)/shard_map/all_gather | solution.py:11
  187.5 2.6 reduce.7
  190.1 83.3 %all-gather.13.cloned.1.call-done = f32[4,1024,256]{2,1,0:T(8,128)} async-done(((f32[1,1024,256]{2,1,0:T(8,128)}), f32[4,1024,256]{2,1,0:T(8,128)}) %all-gather.13.cloned.1.call-update) | async-done | bytes 4194320 | tf_op jit(solution)/shard_map/all_gather | solution.py:11
  273.5 2.6 reduce.6
  276.0 4.2 fusion.7
  280.3 4.2 fusion.6
  284.5 3.6 fusion.5
  288.1 71.1 %all-gather.9.cloned.1.call-done = f32[4,1024,256]{2,1,0:T(8,128)} async-done(((f32[1,1024,256]{2,1,0:T(8,128)}), f32[4,1024,256]{2,1,0:T(8,128)}) %all-gather.9.cloned.1.call-update) | async-done | bytes 4194320 | tf_op jit(solution)/shard_map/all_gather | solution.py:11
  359.2 2.6 reduce.4
  361.8 0.0 copy-start
  361.8 0.0 copy-start.1
  361.8 3.5 fusion.4
  365.3 0.0 copy-done
  365.3 0.0 copy-done.1
  365.3 0.1 pad_maximum_fusion
  365.5 2.0 copy.9
  367.5 0.0 copy-start.3
  367.5 0.0 all-reduce.3.cloned.1.call-update
  367.5 0.6 copy-done.3
  368.1 0.6 dynamic-slice
  369.4 0.1 and_convert_fusion.1
  369.5 791.6 %all-reduce.3.cloned.1.call-done = f32[512,4,256]{0,1,2:T(4,128)} async-done(((f32[512,4,256]{0,1,2:T(4,128)}), f32[512,4,256]{0,1,2:T(4,128)}) %all-reduce.3.cloned.1.call-update) | async-done | bytes 2097168
  1161.0 0.8 dynamic-slice_multiply_fusion
  1161.9 0.6 copy.10
  (2 shorter events, 0.0 us)
Async XLA Ops:
  6.5 95.1 %all-gather.11.cloned.1.call-start = ((), (), s32[]{:S(2)}) async-start(), calls=%async_computation.1 | async-start | bytes 5242880 | tf_op jit(solution)/shard_map/all_gather | solution.py:11
  13.9 2.2 copy-start.2
  14.0 173.6 %all-gather.15.cloned.1.call-start = ((), (), s32[]{:S(2)}) async-start(), calls=%async_computation.3 | async-start | bytes 5242880 | tf_op jit(solution)/shard_map/all_gather | solution.py:11
  14.7 258.7 %all-gather.13.cloned.1.call-start = ((), (), s32[]{:S(2)}) async-start(), calls=%async_computation.2 | async-start | bytes 5242880 | tf_op jit(solution)/shard_map/all_gather | solution.py:11
  15.4 343.8 %all-gather.9.cloned.1.call-start = ((), (), s32[]{:S(2)}) async-start(), calls=%async_computation | async-start | bytes 5242880 | tf_op jit(solution)/shard_map/all_gather | solution.py:11
  16.0 1145.0 %all-reduce.3.cloned.1.call-start = ((), (), s32[]{:S(2)}) async-start(), calls=%async_computation.4 | async-start | bytes 4194304
  361.8 3.5 copy-start
  361.8 3.5 copy-start.1
  367.5 0.7 copy-start.3
Sparse Core Ops, SparseCore 0:
  14.1 87.5 all-gather.10
  103.4 84.0 all-gather.14
  189.4 84.0 all-gather.12
  275.1 84.0 all-gather.8
  367.6 793.3 all-reduce.2
